TPU v7x, 32 devices: a whole 2x2x4 slice. The times are simulated.
32 devices in a mesh: ctx: 8 (over y, x, core), head: 4 (over z).
Axes of the slice: x: 2, y: 2, z: 4, core: 2. Of those that a mesh axis runs over, the one named last changes fastest.
Arguments:
- q_nope: bfloat16 [512, 8192], P('ctx', 'head'), may hold values from -0.59765625 to 0.59765625
- q_rope: bfloat16 [512, 4096], P('ctx', 'head'), may hold values from -6 to 6
- w_uk: bfloat16 [64, 128, 512], P('head'), may hold values from -0.5 to 0.5
- w_uv: bfloat16 [64, 512, 128], P('head'), may hold values from -0.25 to 0.25
- w_o: bfloat16 [8192, 7168], P('head'), may hold values from -0.0625 to 0.0625
- latent_cache: bfloat16 [576, 8192], P(None, 'ctx'), may hold values from -36 to 36
- group_start: int32 [1], replicated, may hold values from 2048 to 7680
Outputs:
- attention_out: bfloat16 [512, 7168], P('ctx', 'head')
All inputs are finite; a program needn't handle non-finite values.
Results may differ from a plain program's by a relative error of at most 0.02.
Values may be sent and summed in bfloat16 or wider, within the bound.
A program may use at most 128 MiB of HBM per device.

v0:
```python
import math
import jax
import jax.numpy as jnp
from jax import lax
from jax.sharding import PartitionSpec as P

LATENT = 512
ROPE = 64
NOPE = 128
VDIM = 128
masked_score = -1e30


def score_scale():
    return (NOPE + ROPE) ** (-0.5) * (0.1 * math.log(32.0) + 1.0) ** 2


def absorb_queries(q_nope, q_rope, w_uk):
    local_heads = w_uk.shape[0]
    tokens_here = q_nope.shape[0]
    nope_part = q_nope.reshape(tokens_here, local_heads, NOPE)
    latent_query = jnp.einsum(
        "thn,hnl->thl", nope_part, w_uk, preferred_element_type=jnp.float32
    ).astype(jnp.bfloat16)
    rope_part = q_rope.reshape(tokens_here, local_heads, ROPE)
    return jnp.concatenate([latent_query, rope_part], axis=2)


def block_scores_of(query_rows, row_position, key_block, key_start):
    scores = jnp.dot(query_rows, key_block, preferred_element_type=jnp.float32) * score_scale()
    key_position = key_start + jnp.arange(key_block.shape[1], dtype=jnp.int32)
    visible = key_position[None, :] <= row_position[:, None]
    return (jnp.where(visible, scores, masked_score), visible)


def latent_product(weights, key_block):
    return lax.dot_general(
        weights.astype(jnp.bfloat16),
        key_block[:LATENT],
        (((1,), (1,)), ((), ())),
        preferred_element_type=jnp.float32,
    )


def online_update(running, query_rows, row_position, key_block, key_start):
    best_sofar, denominator, numerator = running
    scores, visible = block_scores_of(query_rows, row_position, key_block, key_start)
    new_best = jnp.maximum(best_sofar, jnp.max(scores, axis=1))
    decay_factor = jnp.exp(best_sofar - new_best)
    weights = jnp.where(visible, jnp.exp(scores - new_best[:, None]), 0.0)
    denominator = denominator * decay_factor + jnp.sum(weights, axis=1)
    numerator = numerator * decay_factor[:, None] + latent_product(weights, key_block)
    return (new_best, denominator, numerator)


def value_heads(latent_out, w_uv):
    leading = latent_out.astype(jnp.bfloat16)
    remainder = (latent_out - leading.astype(jnp.float32)).astype(jnp.bfloat16)
    first_term = jnp.einsum("thl,hlv->thv", leading, w_uv, preferred_element_type=jnp.float32)
    second_term = jnp.einsum("thl,hlv->thv", remainder, w_uv, preferred_element_type=jnp.float32)
    return first_term + second_term


def on_device(q_nope, q_rope, w_uk, w_uv, w_o, latent_cache, group_start):
    local_heads = w_uk.shape[0]
    tokens_here = q_nope.shape[0]
    queries = absorb_queries(q_nope, q_rope, w_uk)
    query_width = queries.shape[2]
    query_rows = queries.reshape(tokens_here * local_heads, query_width)
    first_token = group_start[0] + lax.axis_index("ctx") * tokens_here
    token_position = first_token + jnp.arange(tokens_here, dtype=jnp.int32)
    row_position = jnp.repeat(token_position, local_heads)
    last_position = first_token + tokens_here - 1
    row_total = query_rows.shape[0]
    initial = (
        jnp.full((row_total,), masked_score, jnp.float32),
        jnp.zeros((row_total,), jnp.float32),
        jnp.zeros((row_total, LATENT), jnp.float32),
    )
    cache_piece = lax.all_gather(latent_cache, "ctx", axis=1, tiled=True)
    span_keys = cache_piece.shape[1]
    step_keys = math.gcd(span_keys, 1024)

    def advance(position, current):
        key_block = lax.dynamic_slice_in_dim(cache_piece, position * step_keys, step_keys, 1)
        key_start = position * step_keys
        return lax.cond(
            key_start <= last_position,
            lambda held_state: online_update(
                held_state, query_rows, row_position, key_block, key_start
            ),
            lambda held_state: held_state,
            current,
        )

    best_all, denominator, numerator = lax.fori_loop(0, span_keys // step_keys, advance, initial)
    latent_out = (numerator / denominator[:, None]).reshape(tokens_here, local_heads, LATENT)
    head_values = value_heads(latent_out, w_uv)
    head_out = head_values.reshape(tokens_here, local_heads * VDIM).astype(jnp.bfloat16)
    mixed_columns = lax.psum_scatter(
        lax.dot_general(
            w_o, head_out, (((0,), (1,)), ((), ())), preferred_element_type=jnp.float32
        ).astype(jnp.bfloat16),
        "head",
        scatter_dimension=0,
        tiled=True,
    ).astype(jnp.float32)
    return mixed_columns.T.astype(jnp.bfloat16)


def solution(mesh):
    placed = (
        P("ctx", "head"),
        P("ctx", "head"),
        P("head", None, None),
        P("head", None, None),
        P("head", None),
        P(None, "ctx"),
        P(),
    )
    return jax.shard_map(
        on_device, mesh=mesh, in_specs=placed, out_specs=P("ctx", "head"), check_vma=False
    )
```

profile of v0, /device:TPU:0, one launch (start us, length us, event | category | flops | bytes accessed | tf_op | source)
XLA Modules:
  0.0 189.2 jit_solution(10341991162294786922)
XLA Ops:
  6.5 0.7 all-gather.2.cloned.1.call-update
  8.0 1.1 concatenate.9
  9.1 1.4 fusion.20
  10.5 0.6 copy.12
  11.1 1.2 pad_maximum_fusion
  12.3 58.4 %all-gather.2.cloned.1.call-done = bf16[576,8192]{1,0:T(8,128)(2,1)} async-done(((bf16[576,1024]{1,0:T(8,128)(2,1)}), bf16[576,8192]{1,0:T(8,128)(2,1)}) %all-gather.2.cloned.1.call-update) | async-done | bytes 9437200 | tf_op jit(solution)/shard_map/all_gather | solution.py:80
  70.7 1.6 broadcast_in_dim.29
  72.3 57.2 %while.18 = (s32[]{:T(128)}, f32[1024]{0:T(1024)S(1)}, f32[1024]{0:T(1024)S(1)}, f32[1024,512]{1,0:T(8,128)}, s32[]{:T(128)}, /*index=5*/bf16[576,8192]{1,0:T(8,...) while((s32[]{:T(128)}, f32[1024]{0:T(1024)S(1)}, ...), condition=%wide.region_5.6_spmd.clone, body=%wide.region_0.5_spmd.clone.sunk | while | flops 2299530240 | bytes 37069400 | solution.py:96
  72.3 9.5 %conditional.3 = ((f32[1024]{0:T(1024)S(1)}, f32[1024]{0:T(1024)S(1)}, f32[1024,512]{1,0:T(8,128)})) conditional(s32[]{:T(128)} %convert_element_type.82, (f32[1024]{0:T(1024)S(1)}, f32[1024]{0:T(1024)S(1)}, f32[1024,512]{1,0:T(8,128)}) %tuple.50, (s32[]{:T(128)}, s32[64]{0:T(128)S(1)}, bf16[576,8192]{1,0:T(8,128)(2,1)}, ...), branch_computations={%region_1.0_spmd, %region_2.4_spmd} | conditional | flops 2299530240 | bytes 37069192 | solution.py:87
  72.3 0.1 le.27
  72.4 3.4 %fusion.2 = (f32[1024]{0:T(1024)S(1)}, f32[1024,1024]{1,0:T(8,128)S(1)}) fusion(s32[1024]{0:T(1024)S(1)} %le.27, s32[1024]{0:T(1024)S(1)} %iota_add_fusion, bf16[1024,576]{1,0:T(8,128)(2,1)S(1)} %get-tuple-element.214, bf16[576,8192]{1,0:T(8,128)(2,1)} %get-tuple-element.213, s32[]{:T(128)S(6)} %select_n.18), kind=kOutput, calls=%fused_computation.3 | convolution fusion | flops 1212152832 | bytes 6565892 | tf_op jit(solution)/shard_map/while/body/eval_jaxpr/cond/branch_1_fun/dot_general | solution.py:30
  75.9 1.5 fusion.4
  77.5 3.0 %multiply_add_fusion = f32[1024,512]{1,0:T(8,128)S(1)} fusion(f32[1024,512]{1,0:T(8,128)S(1)} %copy-done.1, f32[1024,1024]{1,0:T(8,128)S(1)} %get-tuple-element.275, f32[1024]{0:T(1024)S(1)} %max.4, s32[1024]{0:T(1024)S(1)} %le.27, s32[1024]{0:T(1024)S(1)} %iota_add_fusion, bf16[576,8192]{1,0:T(8,128)(2,1)} %get-tuple-element.213, s32[]{:T(128)S(6)} %select_n.18, ...), kind=kOutput, calls=%fused_computation.6 | convolution fusion | flops 1081081856 | bytes 9453572 | tf_op jit(solution)/shard_map/while/body/eval_jaxpr/cond/branch_1_fun/dot_general | solution.py:37
  80.5 1.3 copy-done.2
  81.8 9.5 %conditional.3 = ((f32[1024]{0:T(1024)S(1)}, f32[1024]{0:T(1024)S(1)}, f32[1024,512]{1,0:T(8,128)})) conditional(s32[]{:T(128)} %convert_element_type.82, (f32[1024]{0:T(1024)S(1)}, f32[1024]{0:T(1024)S(1)}, f32[1024,512]{1,0:T(8,128)}) %tuple.50, (s32[]{:T(128)}, s32[64]{0:T(128)S(1)}, bf16[576,8192]{1,0:T(8,128)(2,1)}, ...), branch_computations={%region_1.0_spmd, %region_2.4_spmd} | conditional | flops 2299530240 | bytes 37069192 | solution.py:87
  81.9 0.1 le.27
  82.0 3.4 %fusion.2 = (f32[1024]{0:T(1024)S(1)}, f32[1024,1024]{1,0:T(8,128)S(1)}) fusion(s32[1024]{0:T(1024)S(1)} %le.27, s32[1024]{0:T(1024)S(1)} %iota_add_fusion, bf16[1024,576]{1,0:T(8,128)(2,1)S(1)} %get-tuple-element.214, bf16[576,8192]{1,0:T(8,128)(2,1)} %get-tuple-element.213, s32[]{:T(128)S(6)} %select_n.18), kind=kOutput, calls=%fused_computation.3 | convolution fusion | flops 1212152832 | bytes 6565892 | tf_op jit(solution)/shard_map/while/body/eval_jaxpr/cond/branch_1_fun/dot_general | solution.py:30
  85.4 1.5 fusion.4
  87.0 3.0 %multiply_add_fusion = f32[1024,512]{1,0:T(8,128)S(1)} fusion(f32[1024,512]{1,0:T(8,128)S(1)} %copy-done.1, f32[1024,1024]{1,0:T(8,128)S(1)} %get-tuple-element.275, f32[1024]{0:T(1024)S(1)} %max.4, s32[1024]{0:T(1024)S(1)} %le.27, s32[1024]{0:T(1024)S(1)} %iota_add_fusion, bf16[576,8192]{1,0:T(8,128)(2,1)} %get-tuple-element.213, s32[]{:T(128)S(6)} %select_n.18, ...), kind=kOutput, calls=%fused_computation.6 | convolution fusion | flops 1081081856 | bytes 9453572 | tf_op jit(solution)/shard_map/while/body/eval_jaxpr/cond/branch_1_fun/dot_general | solution.py:37
  90.0 1.3 copy-done.2
  91.3 9.5 %conditional.3 = ((f32[1024]{0:T(1024)S(1)}, f32[1024]{0:T(1024)S(1)}, f32[1024,512]{1,0:T(8,128)})) conditional(s32[]{:T(128)} %convert_element_type.82, (f32[1024]{0:T(1024)S(1)}, f32[1024]{0:T(1024)S(1)}, f32[1024,512]{1,0:T(8,128)}) %tuple.50, (s32[]{:T(128)}, s32[64]{0:T(128)S(1)}, bf16[576,8192]{1,0:T(8,128)(2,1)}, ...), branch_computations={%region_1.0_spmd, %region_2.4_spmd} | conditional | flops 2299530240 | bytes 37069192 | solution.py:87
  91.5 3.4 %fusion.2 = (f32[1024]{0:T(1024)S(1)}, f32[1024,1024]{1,0:T(8,128)S(1)}) fusion(s32[1024]{0:T(1024)S(1)} %le.27, s32[1024]{0:T(1024)S(1)} %iota_add_fusion, bf16[1024,576]{1,0:T(8,128)(2,1)S(1)} %get-tuple-element.214, bf16[576,8192]{1,0:T(8,128)(2,1)} %get-tuple-element.213, s32[]{:T(128)S(6)} %select_n.18), kind=kOutput, calls=%fused_computation.3 | convolution fusion | flops 1212152832 | bytes 6565892 | tf_op jit(solution)/shard_map/while/body/eval_jaxpr/cond/branch_1_fun/dot_general | solution.py:30
  95.0 1.5 fusion.4
  96.6 3.0 %multiply_add_fusion = f32[1024,512]{1,0:T(8,128)S(1)} fusion(f32[1024,512]{1,0:T(8,128)S(1)} %copy-done.1, f32[1024,1024]{1,0:T(8,128)S(1)} %get-tuple-element.275, f32[1024]{0:T(1024)S(1)} %max.4, s32[1024]{0:T(1024)S(1)} %le.27, s32[1024]{0:T(1024)S(1)} %iota_add_fusion, bf16[576,8192]{1,0:T(8,128)(2,1)} %get-tuple-element.213, s32[]{:T(128)S(6)} %select_n.18, ...), kind=kOutput, calls=%fused_computation.6 | convolution fusion | flops 1081081856 | bytes 9453572 | tf_op jit(solution)/shard_map/while/body/eval_jaxpr/cond/branch_1_fun/dot_general | solution.py:37
  99.6 1.3 copy-done.2
  100.9 9.5 %conditional.3 = ((f32[1024]{0:T(1024)S(1)}, f32[1024]{0:T(1024)S(1)}, f32[1024,512]{1,0:T(8,128)})) conditional(s32[]{:T(128)} %convert_element_type.82, (f32[1024]{0:T(1024)S(1)}, f32[1024]{0:T(1024)S(1)}, f32[1024,512]{1,0:T(8,128)}) %tuple.50, (s32[]{:T(128)}, s32[64]{0:T(128)S(1)}, bf16[576,8192]{1,0:T(8,128)(2,1)}, ...), branch_computations={%region_1.0_spmd, %region_2.4_spmd} | conditional | flops 2299530240 | bytes 37069192 | solution.py:87
  101.0 0.1 le.27
  101.0 3.4 %fusion.2 = (f32[1024]{0:T(1024)S(1)}, f32[1024,1024]{1,0:T(8,128)S(1)}) fusion(s32[1024]{0:T(1024)S(1)} %le.27, s32[1024]{0:T(1024)S(1)} %iota_add_fusion, bf16[1024,576]{1,0:T(8,128)(2,1)S(1)} %get-tuple-element.214, bf16[576,8192]{1,0:T(8,128)(2,1)} %get-tuple-element.213, s32[]{:T(128)S(6)} %select_n.18), kind=kOutput, calls=%fused_computation.3 | convolution fusion | flops 1212152832 | bytes 6565892 | tf_op jit(solution)/shard_map/while/body/eval_jaxpr/cond/branch_1_fun/dot_general | solution.py:30
  104.5 1.5 fusion.4
  106.1 3.0 %multiply_add_fusion = f32[1024,512]{1,0:T(8,128)S(1)} fusion(f32[1024,512]{1,0:T(8,128)S(1)} %copy-done.1, f32[1024,1024]{1,0:T(8,128)S(1)} %get-tuple-element.275, f32[1024]{0:T(1024)S(1)} %max.4, s32[1024]{0:T(1024)S(1)} %le.27, s32[1024]{0:T(1024)S(1)} %iota_add_fusion, bf16[576,8192]{1,0:T(8,128)(2,1)} %get-tuple-element.213, s32[]{:T(128)S(6)} %select_n.18, ...), kind=kOutput, calls=%fused_computation.6 | convolution fusion | flops 1081081856 | bytes 9453572 | tf_op jit(solution)/shard_map/while/body/eval_jaxpr/cond/branch_1_fun/dot_general | solution.py:37
  109.1 1.3 copy-done.2
  110.4 9.5 %conditional.3 = ((f32[1024]{0:T(1024)S(1)}, f32[1024]{0:T(1024)S(1)}, f32[1024,512]{1,0:T(8,128)})) conditional(s32[]{:T(128)} %convert_element_type.82, (f32[1024]{0:T(1024)S(1)}, f32[1024]{0:T(1024)S(1)}, f32[1024,512]{1,0:T(8,128)}) %tuple.50, (s32[]{:T(128)}, s32[64]{0:T(128)S(1)}, bf16[576,8192]{1,0:T(8,128)(2,1)}, ...), branch_computations={%region_1.0_spmd, %region_2.4_spmd} | conditional | flops 2299530240 | bytes 37069192 | solution.py:87
  110.5 0.1 le.27
  110.6 3.4 %fusion.2 = (f32[1024]{0:T(1024)S(1)}, f32[1024,1024]{1,0:T(8,128)S(1)}) fusion(s32[1024]{0:T(1024)S(1)} %le.27, s32[1024]{0:T(1024)S(1)} %iota_add_fusion, bf16[1024,576]{1,0:T(8,128)(2,1)S(1)} %get-tuple-element.214, bf16[576,8192]{1,0:T(8,128)(2,1)} %get-tuple-element.213, s32[]{:T(128)S(6)} %select_n.18), kind=kOutput, calls=%fused_computation.3 | convolution fusion | flops 1212152832 | bytes 6565892 | tf_op jit(solution)/shard_map/while/body/eval_jaxpr/cond/branch_1_fun/dot_general | solution.py:30
  114.0 1.5 fusion.4
  115.6 3.0 %multiply_add_fusion = f32[1024,512]{1,0:T(8,128)S(1)} fusion(f32[1024,512]{1,0:T(8,128)S(1)} %copy-done.1, f32[1024,1024]{1,0:T(8,128)S(1)} %get-tuple-element.275, f32[1024]{0:T(1024)S(1)} %max.4, s32[1024]{0:T(1024)S(1)} %le.27, s32[1024]{0:T(1024)S(1)} %iota_add_fusion, bf16[576,8192]{1,0:T(8,128)(2,1)} %get-tuple-element.213, s32[]{:T(128)S(6)} %select_n.18, ...), kind=kOutput, calls=%fused_computation.6 | convolution fusion | flops 1081081856 | bytes 9453572 | tf_op jit(solution)/shard_map/while/body/eval_jaxpr/cond/branch_1_fun/dot_general | solution.py:37
  118.7 1.3 copy-done.2
  120.0 9.5 %conditional.3 = ((f32[1024]{0:T(1024)S(1)}, f32[1024]{0:T(1024)S(1)}, f32[1024,512]{1,0:T(8,128)})) conditional(s32[]{:T(128)} %convert_element_type.82, (f32[1024]{0:T(1024)S(1)}, f32[1024]{0:T(1024)S(1)}, f32[1024,512]{1,0:T(8,128)}) %tuple.50, (s32[]{:T(128)}, s32[64]{0:T(128)S(1)}, bf16[576,8192]{1,0:T(8,128)(2,1)}, ...), branch_computations={%region_1.0_spmd, %region_2.4_spmd} | conditional | flops 2299530240 | bytes 37069192 | solution.py:87
  120.1 3.4 %fusion.2 = (f32[1024]{0:T(1024)S(1)}, f32[1024,1024]{1,0:T(8,128)S(1)}) fusion(s32[1024]{0:T(1024)S(1)} %le.27, s32[1024]{0:T(1024)S(1)} %iota_add_fusion, bf16[1024,576]{1,0:T(8,128)(2,1)S(1)} %get-tuple-element.214, bf16[576,8192]{1,0:T(8,128)(2,1)} %get-tuple-element.213, s32[]{:T(128)S(6)} %select_n.18), kind=kOutput, calls=%fused_computation.3 | convolution fusion | flops 1212152832 | bytes 6565892 | tf_op jit(solution)/shard_map/while/body/eval_jaxpr/cond/branch_1_fun/dot_general | solution.py:30
  123.6 1.5 fusion.4
  125.2 3.0 %multiply_add_fusion = f32[1024,512]{1,0:T(8,128)S(1)} fusion(f32[1024,512]{1,0:T(8,128)S(1)} %copy-done.1, f32[1024,1024]{1,0:T(8,128)S(1)} %get-tuple-element.275, f32[1024]{0:T(1024)S(1)} %max.4, s32[1024]{0:T(1024)S(1)} %le.27, s32[1024]{0:T(1024)S(1)} %iota_add_fusion, bf16[576,8192]{1,0:T(8,128)(2,1)} %get-tuple-element.213, s32[]{:T(128)S(6)} %select_n.18, ...), kind=kOutput, calls=%fused_computation.6 | convolution fusion | flops 1081081856 | bytes 9453572 | tf_op jit(solution)/shard_map/while/body/eval_jaxpr/cond/branch_1_fun/dot_general | solution.py:37
  128.2 1.3 copy-done.2
  129.5 1.9 %broadcast_divide_fusion = f32[1024,512]{1,0:T(8,128)S(1)} fusion(f32[1024,512]{1,0:T(8,128)} %get-tuple-element.231, f32[1024]{0:T(1024)S(1)} %get-tuple-element.232), kind=kLoop, calls=%fused_computation.31 | loop fusion | flops 524288 | bytes 4198400 | tf_op jit(solution)/shard_map/div | solution.py:97
  131.5 0.3 copy-done.3
  131.7 1.3 fusion.19
  133.0 1.3 fusion.22
  134.4 13.1 %fusion.18 = bf16[7168,64]{0,1:T(8,128)(2,1)} fusion(bf16[2048,7168]{1,0:T(8,128)(2,1)} %param.15, bf16[16,8,8,128]{3,2,1,0:T(8,128)(2,1)S(1)} %fusion.22), kind=kOutput, calls=%fused_computation.21 | convolution fusion | flops 1879506944 | bytes 30539776 | tf_op jit(solution)/shard_map/dot_general | solution.py:101
  147.5 34.9 %reduce-scatter.2.cloned.1.call-done = bf16[1792,64]{0,1:T(8,128)(2,1)} async-done(((bf16[7168,64]{0,1:T(8,128)(2,1)}), bf16[1792,64]{0,1:T(8,128)(2,1)}) %reduce-scatter.2.cloned.1.call-update) | async-done | bytes 229392 | tf_op jit(solution)/shard_map/reduce_scatter | solution.py:100
  (63 shorter events, 0.9 us)
Async XLA Ops:
  6.5 2.5 %copy-start = (bf16[16,128,512]{2,1,0:T(8,128)(2,1)S(1)}, bf16[16,128,512]{2,1,0:T(8,128)(2,1)}, u32[]{:S(2)}) copy-start(bf16[16,128,512]{2,1,0:T(8,128)(2,1)} %param.13) | copy-start | bytes 6291460
  6.5 64.2 %all-gather.2.cloned.1.call-start = ((), (), s32[]{:S(2)}) async-start(), calls=%async_computation.1 | async-start | bytes 10616832 | tf_op jit(solution)/shard_map/all_gather | solution.py:80
  7.3 175.1 %reduce-scatter.2.cloned.1.call-start = ((), (), s32[]{:S(2)}) async-start(), calls=%async_computation.2 | async-start | bytes 1146880 | tf_op jit(solution)/shard_map/reduce_scatter | solution.py:100
  12.3 60.0 %copy-start.4 = (bf16[1024,576]{1,0:T(8,128)(2,1)S(1)}, bf16[1024,576]{1,0:T(8,128)(2,1)}, u32[]{:S(2)}) copy-start(bf16[1024,576]{1,0:T(8,128)(2,1)} %pad_maximum_fusion) | copy-start | bytes 3538948
  75.9 1.6 copy-start.1
  80.5 1.3 copy-start.2
  85.4 1.6 copy-start.1
  90.0 1.3 copy-start.2
  95.0 1.6 copy-start.1
  99.6 1.3 copy-start.2
  104.5 1.6 copy-start.1
  109.1 1.3 copy-start.2
  114.0 1.6 copy-start.1
  118.6 1.3 copy-start.2
  123.6 1.6 copy-start.1
  128.2 1.3 copy-start.2
  129.5 2.2 %copy-start.3 = (bf16[16,512,128]{2,1,0:T(8,128)(2,1)S(1)}, bf16[16,512,128]{2,1,0:T(8,128)(2,1)}, u32[]{:S(2)}) copy-start(bf16[16,512,128]{2,1,0:T(8,128)(2,1)} %param.14) | copy-start | bytes 6291460
Sparse Core Ops, SparseCore 0:
  9.2 61.4 all-gather.1
  147.6 34.7 reduce-scatter.1
where the time goes:
time: 190 us; the launch traced here: 189 us
  waiting for transfers between devices  94 us (49%)
  matrix products  55.8 us (29%)
  between operations  14.1 us (7%)
  other arithmetic  12.5 us (7%)
  local copies, waits for them, and re-layouts  12.4 us (7%)
    all_gather x1, waiting for transfers between devices, on_device(): cache_piece = lax.all_gather(latent_cache, 'ctx', axis=1, tiled=True)  58.4 us
    reduce_scatter x1, waiting for transfers between devices, on_device(): lax.psum_scatter(lax.dot_general(w_o, head_out, (((0,), (1,)), ((), ())),...  34.9 us
    dot_general x6, matrix products, block_scores_of(): jnp.dot(query_rows, key_block, preferred_element_type=jnp.float32)  20.6 us
    dot_general x6, matrix products, latent_product(): lax.dot_general(weights.astype(jnp.bfloat16), key_block[:LATENT], (((1,),...  18.1 us
    dot_general x1, matrix products, on_device(): lax.dot_general(w_o, head_out, (((0,), (1,)), ((), ())), preferred_elemen...  13.1 us
    reduce_sum x6, other arithmetic, online_update(): denominator = denominator * decay_factor + jnp.sum(weights, axis=1)  9.27 us
    cond x30, local copies, waits for them, and re-layouts  7.95 us
  transfers between devices with their start and end apart: 2, of which 2 were waited for; matrix products, arithmetic and copies ran while one was open for 2% of the time, Pallas kernels for 0%

commit v1 on v0

--- a/solution.py
+++ b/solution.py
@@ -9,6 +9,24 @@
 NOPE = 128
 VDIM = 128
 masked_score = -1e30
+
+
+def in_order(parts, dim):
+    parts = jnp.moveaxis(parts, 0, dim)
+    shape = parts.shape
+    return parts.reshape(*shape[:dim], shape[dim] * shape[dim + 1], *shape[dim + 2 :])
+
+
+def doubled(shard, axis):
+    size = lax.axis_size(axis)
+    blocks = shard[None]
+    for level in range(size.bit_length() - 1):
+        bit = 1 << level
+        other = lax.ppermute(blocks, axis, [(i, i ^ bit) for i in range(size)])
+        both = jnp.stack([blocks, other])
+        upper = lax.axis_index(axis) >> level & 1
+        blocks = jnp.where(upper == 0, both, both[::-1]).reshape(-1, *shard.shape)
+    return blocks
 
 
 def score_scale():
@@ -77,7 +95,7 @@
         jnp.zeros((row_total,), jnp.float32),
         jnp.zeros((row_total, LATENT), jnp.float32),
     )
-    cache_piece = lax.all_gather(latent_cache, "ctx", axis=1, tiled=True)
+    cache_piece = in_order(doubled(latent_cache, "ctx"), 1)
     span_keys = cache_piece.shape[1]
     step_keys = math.gcd(span_keys, 1024)
 

time: 190 us -> 323 us (1.70)
  waiting for transfers between devices: 94 us -> 189 us
  other arithmetic: 12.5 us -> 46.1 us
  starting transfers between devices: 0.04 us -> 5.11 us
    ppermute x0 -> x3, waiting for transfers between devices: none -> 154 us  [doubled(): other = lax.ppermute(blocks, axis, [(i, i ^ bit) for i in range(size)])]
    all_gather x1 -> x0, waiting for transfers between devices: 58.4 us -> none  [on_device(): cache_piece = lax.all_gather(latent_cache, 'ctx', axis=1, tiled=True)]
    select_n x0 -> x2, other arithmetic: none -> 19.1 us  [doubled(): blocks = jnp.where(upper == 0, both, both[::-1]).reshape(-1, *shard.shape)]
    another operation x0 -> x4, other arithmetic: none -> 15.7 us  [doubled(): both = jnp.stack([blocks, other])]
    unnamed x6 -> x13, local copies, waits for them, and re-layouts: 0.27 us -> 10.3 us
    cond x30 -> x6, local copies, waits for them, and re-layouts: 7.95 us -> 0.02 us
    ppermute x0 -> x3, starting transfers between devices: none -> 5.11 us  [doubled(): other = lax.ppermute(blocks, axis, [(i, i ^ bit) for i in range(size)])]
  transfers between devices with their start and end apart: 2 -> 4, of which waited for: 2 -> 4; matrix products, arithmetic and copies ran while one was open for 2% -> 0% of each run, Pallas kernels for 0% -> 0%
where the time goes in v1:
time: 323 us
  waiting for transfers between devices  189 us (59%)
  matrix products  55.1 us (17%)
  other arithmetic  46.1 us (14%)
  between operations  14.2 us (4%)
  local copies, waits for them, and re-layouts  12.2 us (4%)
  starting transfers between devices  5.11 us (2%)
    ppermute x3, waiting for transfers between devices, doubled(): other = lax.ppermute(blocks, axis, [(i, i ^ bit) for i in range(size)])  154 us
    reduce_scatter x1, waiting for transfers between devices, on_device(): lax.psum_scatter(lax.dot_general(w_o, head_out, (((0,), (1,)), ((), ())),...  34.8 us
    dot_general x6, matrix products, block_scores_of(): jnp.dot(query_rows, key_block, preferred_element_type=jnp.float32)  20.5 us
    select_n x2, other arithmetic, doubled(): blocks = jnp.where(upper == 0, both, both[::-1]).reshape(-1, *shard.shape)  19.1 us
    dot_general x6, matrix products, latent_product(): lax.dot_general(weights.astype(jnp.bfloat16), key_block[:LATENT], (((1,),...  18.1 us
    another operation x4, other arithmetic, doubled(): both = jnp.stack([blocks, other])  15.7 us
    dot_general x1, matrix products, on_device(): lax.dot_general(w_o, head_out, (((0,), (1,)), ((), ())), preferred_elemen...  13.2 us
    unnamed x13, local copies, waits for them, and re-layouts  10.3 us
  transfers between devices with their start and end apart: 4, of which 4 were waited for; matrix products, arithmetic and copies ran while one was open for 0% of the time, Pallas kernels for 0%

profile of v1, /device:TPU:0, one launch (start us, length us, event | category | flops | bytes accessed | tf_op | source)
XLA Modules:
  0.0 322.8 jit_solution(6539666358499795412)
XLA Ops:
  6.5 0.5 collective-permute-start
  7.0 2.7 collective-permute-done
  9.7 1.5 pad_maximum_fusion.2
  11.2 3.1 fusion.20
  14.3 2.8 collective-permute-start.1
  17.2 51.9 %collective-permute-done.1 = bf16[2,576,1024]{2,1,0:T(8,128)(2,1)} collective-permute-done((bf16[2,576,1024]{2,1,0:T(8,128)(2,1)}, bf16[2,576,1024]{2,1,0:T(8,128)(2,1)}, u32[]{:S(2)}, u32[]{:S(2)}) %collective-permute-start.1) | collective-permute-done | bytes 2359328 | tf_op jit(solution)/shard_map/ppermute | solution.py:25
  69.1 2.8 pad_maximum_fusion.1
  71.9 3.6 %reverse_select_fusion.1 = bf16[2,2,576,1024]{3,2,1,0:T(8,128)(2,1)} fusion(bf16[2,2,576,1024]{3,2,1,0:T(8,128)(2,1)S(1)} %pad_maximum_fusion.1, pred[]{:T(512)S(6)} %eq.10), kind=kLoop, calls=%fused_computation.24 | loop fusion | flops 2359296 | bytes 9437185 | tf_op jit(solution)/shard_map/jit(_where)/select_n | solution.py:28
  75.5 1.8 collective-permute-start.2
  77.9 0.4 fusion.22
  78.4 0.6 copy.14
  79.0 0.2 concatenate.9
  79.3 99.8 %collective-permute-done.2 = bf16[4,576,1024]{2,1,0:T(8,128)(2,1)} collective-permute-done((bf16[4,576,1024]{2,1,0:T(8,128)(2,1)}, bf16[4,576,1024]{2,1,0:T(8,128)(2,1)}, u32[]{:S(2)}, u32[]{:S(2)}) %collective-permute-start.2) | collective-permute-done | bytes 4718624 | tf_op jit(solution)/shard_map/ppermute | solution.py:25
  179.1 8.3 %pad_maximum_fusion = bf16[2,4,576,1024]{3,2,1,0:T(8,128)(2,1)} fusion(bf16[1,4,576,1024]{3,2,1,0:T(8,128)(2,1)} %bitcast.10, bf16[1,4,576,1024]{3,2,1,0:T(8,128)(2,1)} %bitcast.8), kind=kLoop, calls=%fused_computation.21 | loop fusion | flops 4718592 | bytes 18874368 | tf_op jit(solution)/shard_map/stack | solution.py:26
  187.3 15.5 %reverse_select_fusion = bf16[2,4,576,1024]{3,2,1,0:T(8,128)(2,1)} fusion(bf16[2,4,576,1024]{3,2,1,0:T(8,128)(2,1)} %pad_maximum_fusion, pred[]{:T(512)S(6)} %eq.9), kind=kLoop, calls=%fused_computation.20 | loop fusion | flops 4718592 | bytes 18874368 | tf_op jit(solution)/shard_map/jit(_where)/select_n | solution.py:28
  202.8 9.0 %copy.21 = bf16[72,8,8,1024]{3,1,2,0:T(8,128)(2,1)} copy(bf16[72,8,8,1024]{3,1,0,2:T(8,128)(2,1)} %bitcast.57) | data formatting | bytes 18874368
  211.8 0.2 broadcast_in_dim.32
  212.1 49.7 %while.18 = (s32[]{:T(128)}, f32[1024]{0:T(1024)S(1)}, f32[1024]{0:T(1024)S(1)}, f32[1024,512]{1,0:T(8,128)S(1)}, s32[]{:T(128)}, /*index=5*/bf16[576,8192]{1,0:...) while((s32[]{:T(128)}, f32[1024]{0:T(1024)S(1)}, ...), condition=%wide.region_5.6_spmd.clone, body=%wide.region_0.5_spmd.clone.sunk | while | flops 2299530240 | bytes 20292124 | solution.py:114
  212.3 8.2 %conditional.3 = ((f32[1024]{0:T(1024)S(1)}, f32[1024]{0:T(1024)S(1)}, f32[1024,512]{1,0:T(8,128)S(1)})) conditional(s32[]{:T(128)} %convert_element_type.82, (f32[1024]{0:T(1024)S(1)}, f32[1024]{0:T(1024)S(1)}, f32[1024,512]{1,0:T(8,128)S(1)}) %tuple.51, (s32[]{:T(128)}, s32[64]{0:T(128)S(1)}, bf16[576,8192]{1,0:T(8,128)(2,1)}, ...), branch_computations={%region_1.1_spmd, %region_2.4_spmd} | conditional | flops 2299530240 | bytes 20291918 | solution.py:105
  212.4 3.4 %fusion.2 = (f32[1024]{0:T(1024)S(1)}, f32[1024,1024]{1,0:T(8,128)S(1)}) fusion(s32[1024]{0:T(1024)S(1)} %le.27, s32[1024]{0:T(1024)S(1)} %iota_add_fusion, bf16[1024,576]{1,0:T(8,128)(2,1)S(1)} %get-tuple-element.214, bf16[576,8192]{1,0:T(8,128)(2,1)} %get-tuple-element.213, s32[]{:T(128)S(6)} %select_n.36), kind=kOutput, calls=%fused_computation.3 | convolution fusion | flops 1212152832 | bytes 6565892 | tf_op jit(solution)/shard_map/while/body/eval_jaxpr/cond/branch_1_fun/dot_general | solution.py:48
  215.9 1.5 fusion.4
  217.4 3.0 multiply_add_fusion
  220.5 8.2 %conditional.3 = ((f32[1024]{0:T(1024)S(1)}, f32[1024]{0:T(1024)S(1)}, f32[1024,512]{1,0:T(8,128)S(1)})) conditional(s32[]{:T(128)} %convert_element_type.82, (f32[1024]{0:T(1024)S(1)}, f32[1024]{0:T(1024)S(1)}, f32[1024,512]{1,0:T(8,128)S(1)}) %tuple.51, (s32[]{:T(128)}, s32[64]{0:T(128)S(1)}, bf16[576,8192]{1,0:T(8,128)(2,1)}, ...), branch_computations={%region_1.1_spmd, %region_2.4_spmd} | conditional | flops 2299530240 | bytes 20291918 | solution.py:105
  220.7 3.4 %fusion.2 = (f32[1024]{0:T(1024)S(1)}, f32[1024,1024]{1,0:T(8,128)S(1)}) fusion(s32[1024]{0:T(1024)S(1)} %le.27, s32[1024]{0:T(1024)S(1)} %iota_add_fusion, bf16[1024,576]{1,0:T(8,128)(2,1)S(1)} %get-tuple-element.214, bf16[576,8192]{1,0:T(8,128)(2,1)} %get-tuple-element.213, s32[]{:T(128)S(6)} %select_n.36), kind=kOutput, calls=%fused_computation.3 | convolution fusion | flops 1212152832 | bytes 6565892 | tf_op jit(solution)/shard_map/while/body/eval_jaxpr/cond/branch_1_fun/dot_general | solution.py:48
  224.1 1.5 fusion.4
  225.7 3.0 multiply_add_fusion
  228.7 8.2 %conditional.3 = ((f32[1024]{0:T(1024)S(1)}, f32[1024]{0:T(1024)S(1)}, f32[1024,512]{1,0:T(8,128)S(1)})) conditional(s32[]{:T(128)} %convert_element_type.82, (f32[1024]{0:T(1024)S(1)}, f32[1024]{0:T(1024)S(1)}, f32[1024,512]{1,0:T(8,128)S(1)}) %tuple.51, (s32[]{:T(128)}, s32[64]{0:T(128)S(1)}, bf16[576,8192]{1,0:T(8,128)(2,1)}, ...), branch_computations={%region_1.1_spmd, %region_2.4_spmd} | conditional | flops 2299530240 | bytes 20291918 | solution.py:105
  228.9 3.4 %fusion.2 = (f32[1024]{0:T(1024)S(1)}, f32[1024,1024]{1,0:T(8,128)S(1)}) fusion(s32[1024]{0:T(1024)S(1)} %le.27, s32[1024]{0:T(1024)S(1)} %iota_add_fusion, bf16[1024,576]{1,0:T(8,128)(2,1)S(1)} %get-tuple-element.214, bf16[576,8192]{1,0:T(8,128)(2,1)} %get-tuple-element.213, s32[]{:T(128)S(6)} %select_n.36), kind=kOutput, calls=%fused_computation.3 | convolution fusion | flops 1212152832 | bytes 6565892 | tf_op jit(solution)/shard_map/while/body/eval_jaxpr/cond/branch_1_fun/dot_general | solution.py:48
  232.4 1.5 fusion.4
  233.9 3.0 multiply_add_fusion
  237.0 8.2 %conditional.3 = ((f32[1024]{0:T(1024)S(1)}, f32[1024]{0:T(1024)S(1)}, f32[1024,512]{1,0:T(8,128)S(1)})) conditional(s32[]{:T(128)} %convert_element_type.82, (f32[1024]{0:T(1024)S(1)}, f32[1024]{0:T(1024)S(1)}, f32[1024,512]{1,0:T(8,128)S(1)}) %tuple.51, (s32[]{:T(128)}, s32[64]{0:T(128)S(1)}, bf16[576,8192]{1,0:T(8,128)(2,1)}, ...), branch_computations={%region_1.1_spmd, %region_2.4_spmd} | conditional | flops 2299530240 | bytes 20291918 | solution.py:105
  237.2 3.4 %fusion.2 = (f32[1024]{0:T(1024)S(1)}, f32[1024,1024]{1,0:T(8,128)S(1)}) fusion(s32[1024]{0:T(1024)S(1)} %le.27, s32[1024]{0:T(1024)S(1)} %iota_add_fusion, bf16[1024,576]{1,0:T(8,128)(2,1)S(1)} %get-tuple-element.214, bf16[576,8192]{1,0:T(8,128)(2,1)} %get-tuple-element.213, s32[]{:T(128)S(6)} %select_n.36), kind=kOutput, calls=%fused_computation.3 | convolution fusion | flops 1212152832 | bytes 6565892 | tf_op jit(solution)/shard_map/while/body/eval_jaxpr/cond/branch_1_fun/dot_general | solution.py:48
  240.6 1.5 fusion.4
  242.2 3.0 multiply_add_fusion
  245.2 8.2 %conditional.3 = ((f32[1024]{0:T(1024)S(1)}, f32[1024]{0:T(1024)S(1)}, f32[1024,512]{1,0:T(8,128)S(1)})) conditional(s32[]{:T(128)} %convert_element_type.82, (f32[1024]{0:T(1024)S(1)}, f32[1024]{0:T(1024)S(1)}, f32[1024,512]{1,0:T(8,128)S(1)}) %tuple.51, (s32[]{:T(128)}, s32[64]{0:T(128)S(1)}, bf16[576,8192]{1,0:T(8,128)(2,1)}, ...), branch_computations={%region_1.1_spmd, %region_2.4_spmd} | conditional | flops 2299530240 | bytes 20291918 | solution.py:105
  245.4 3.4 %fusion.2 = (f32[1024]{0:T(1024)S(1)}, f32[1024,1024]{1,0:T(8,128)S(1)}) fusion(s32[1024]{0:T(1024)S(1)} %le.27, s32[1024]{0:T(1024)S(1)} %iota_add_fusion, bf16[1024,576]{1,0:T(8,128)(2,1)S(1)} %get-tuple-element.214, bf16[576,8192]{1,0:T(8,128)(2,1)} %get-tuple-element.213, s32[]{:T(128)S(6)} %select_n.36), kind=kOutput, calls=%fused_computation.3 | convolution fusion | flops 1212152832 | bytes 6565892 | tf_op jit(solution)/shard_map/while/body/eval_jaxpr/cond/branch_1_fun/dot_general | solution.py:48
  248.9 1.5 fusion.4
  250.4 3.0 multiply_add_fusion
  253.5 8.2 %conditional.3 = ((f32[1024]{0:T(1024)S(1)}, f32[1024]{0:T(1024)S(1)}, f32[1024,512]{1,0:T(8,128)S(1)})) conditional(s32[]{:T(128)} %convert_element_type.82, (f32[1024]{0:T(1024)S(1)}, f32[1024]{0:T(1024)S(1)}, f32[1024,512]{1,0:T(8,128)S(1)}) %tuple.51, (s32[]{:T(128)}, s32[64]{0:T(128)S(1)}, bf16[576,8192]{1,0:T(8,128)(2,1)}, ...), branch_computations={%region_1.1_spmd, %region_2.4_spmd} | conditional | flops 2299530240 | bytes 20291918 | solution.py:105
  253.7 3.4 %fusion.2 = (f32[1024]{0:T(1024)S(1)}, f32[1024,1024]{1,0:T(8,128)S(1)}) fusion(s32[1024]{0:T(1024)S(1)} %le.27, s32[1024]{0:T(1024)S(1)} %iota_add_fusion, bf16[1024,576]{1,0:T(8,128)(2,1)S(1)} %get-tuple-element.214, bf16[576,8192]{1,0:T(8,128)(2,1)} %get-tuple-element.213, s32[]{:T(128)S(6)} %select_n.36), kind=kOutput, calls=%fused_computation.3 | convolution fusion | flops 1212152832 | bytes 6565892 | tf_op jit(solution)/shard_map/while/body/eval_jaxpr/cond/branch_1_fun/dot_general | solution.py:48
  257.1 1.5 fusion.4
  258.7 3.0 multiply_add_fusion
  261.8 1.3 copy-done.2
  263.1 1.9 broadcast_divide_fusion
  265.0 1.4 fusion.21
  266.4 1.5 fusion.24
  267.9 13.2 %fusion.18 = bf16[7168,64]{0,1:T(8,128)(2,1)} fusion(bf16[2048,7168]{1,0:T(8,128)(2,1)} %param.15, bf16[16,8,8,128]{3,2,1,0:T(8,128)(2,1)S(1)} %fusion.24), kind=kOutput, calls=%fused_computation.23 | convolution fusion | flops 1879506944 | bytes 30539776 | tf_op jit(solution)/shard_map/dot_general | solution.py:119
  281.2 34.8 %reduce-scatter.2.cloned.1.call-done = bf16[1792,64]{0,1:T(8,128)(2,1)} async-done(((bf16[7168,64]{0,1:T(8,128)(2,1)}), bf16[1792,64]{0,1:T(8,128)(2,1)}) %reduce-scatter.2.cloned.1.call-update) | async-done | bytes 229392 | tf_op jit(solution)/shard_map/reduce_scatter | solution.py:118
  (55 shorter events, 1.2 us)
Async XLA Ops:
  6.5 71.4 %copy-start = (bf16[16,128,512]{2,1,0:T(8,128)(2,1)S(1)}, bf16[16,128,512]{2,1,0:T(8,128)(2,1)}, u32[]{:S(2)}) copy-start(bf16[16,128,512]{2,1,0:T(8,128)(2,1)} %param.13) | copy-start | bytes 6291460
  6.5 309.4 %reduce-scatter.2.cloned.1.call-start = ((), (), s32[]{:S(2)}) async-start(), calls=%async_computation.1 | async-start | bytes 1146880 | tf_op jit(solution)/shard_map/reduce_scatter | solution.py:118
  6.5 3.2 collective-permute-start
  14.3 54.7 %collective-permute-start.1 = (bf16[2,576,1024]{2,1,0:T(8,128)(2,1)}, bf16[2,576,1024]{2,1,0:T(8,128)(2,1)}, u32[]{:S(2)}, u32[]{:S(2)}) collective-permute-start(bf16[2,576,1024]{2,1,0:T(8,128)(2,1)} %get-tuple-element.277), channel_id=1, source_target_pairs={{0,8},{4,12},{8,0},{12,4},{16,24},{20,28},{24,16},{28,20},{1,9},{5... | collective-permute-start | bytes 7077896 | tf_op jit(solution)/shard_map/ppermute | solution.py:25
  71.9 6.0 %copy-start.4 = (bf16[64,2048]{1,0:T(8,128)(2,1)S(1)}, bf16[64,2048]{1,0:T(8,128)(2,1)}, u32[]{:S(2)}) copy-start(bf16[64,2048]{1,0:T(8,128)(2,1)} %param.11) | copy-start | bytes 786436
  75.5 103.6 %collective-permute-start.2 = (bf16[4,576,1024]{2,1,0:T(8,128)(2,1)}, bf16[4,576,1024]{2,1,0:T(8,128)(2,1)}, u32[]{:S(2)}, u32[]{:S(2)}) collective-permute-start(bf16[4,576,1024]{2,1,0:T(8,128)(2,1)} %bitcast.9), channel_id=1, source_target_pairs={{0,16},{4,20},{8,24},{12,28},{16,0},{20,4},{24,8},{28,12},{1,17},{... | collective-permute-start | bytes 14155784 | tf_op jit(solution)/shard_map/ppermute | solution.py:25
  77.9 1.0 copy-start.5
  261.8 1.3 copy-start.2
  261.8 3.2 copy-start.3
  267.9 48.1 %copy-start.1 = (bf16[16,128,512]{2,1,0:T(8,128)(2,1)S(1)}, bf16[16,128,512]{2,1,0:T(8,128)(2,1)}, u32[]{:S(2)}) copy-start(bf16[16,128,512]{2,1,0:T(8,128)(2,1)} %param.13) | copy-start | bytes 6291460
Sparse Core Ops, SparseCore 0:
  281.3 34.6 reduce-scatter.1
